TPU v7x, 256 devices: a whole 4x4x8 slice. The times are simulated.
256 devices in a mesh: row: 8 (over x, core), col: 32 (over z, y).
Axes of the slice: x: 4, y: 4, z: 8, core: 2. Of those that a mesh axis runs over, the one named last changes fastest.
Arguments:
- inputs: bfloat16 [1024, 8192], P('col', 'row'), may hold values from -6 to 6
- target: bfloat16 [1024, 8192], P(None, 'row'), may hold values from -6 to 6
- gate_weight: bfloat16 [8192, 16384], P('row', 'col'), may hold values from -0.0625 to 0.0625
- up_weight: bfloat16 [8192, 16384], P('row', 'col'), may hold values from -0.0625 to 0.0625
- down_weight: bfloat16 [16384, 8192], P('col', 'row'), may hold values from -0.046875 to 0.046875
Outputs:
- output: bfloat16 [1024, 8192], P('col', 'row')
- grad_inputs: bfloat16 [1024, 8192], P('col', 'row')
- grad_gate_weight: bfloat16 [8192, 16384], P('row', 'col')
- grad_up_weight: bfloat16 [8192, 16384], P('row', 'col')
- grad_down_weight: bfloat16 [16384, 8192], P('col', 'row')
All inputs are finite; a program needn't handle non-finite values.
Results may differ from a plain program's by a relative error of at most 0.0065.
Values may be sent and summed in bfloat16 or wider, within the bound.
No kernel may reach another device: no remote copies, remote signals or barrier semaphores. Data moves between devices by JAX's collectives and lax.ppermute only.
A program may use at most 64 MiB of HBM per device.

v0:
```python
import jax
import jax.numpy as jnp
from jax import lax
from jax.sharding import PartitionSpec as P


def contract_first(left, right):
    return lax.dot_general(
        left, right, (((0,), (0,)), ((), ())), preferred_element_type=jnp.float32
    )


def contract_last(left, right):
    return lax.dot_general(
        left, right, (((1,), (1,)), ((), ())), preferred_element_type=jnp.float32
    )


def gate_grads(hidden_grad, gate_act, up_act):
    sigma = jax.nn.sigmoid(gate_act)
    silu_val = gate_act * sigma
    grad_gate = (hidden_grad * up_act * sigma * (1.0 + gate_act * (1.0 - sigma))).astype(
        jnp.bfloat16
    )
    grad_up = (hidden_grad * silu_val).astype(jnp.bfloat16)
    return (grad_gate, grad_up)


def body(inputs, target, gate_weight, up_weight, down_weight):
    tokens_all = lax.all_gather(inputs, "col", axis=0, tiled=True)
    gate_part = jnp.dot(tokens_all, gate_weight, preferred_element_type=jnp.float32)
    up_part = jnp.dot(tokens_all, up_weight, preferred_element_type=jnp.float32)
    gate_own, up_own = (
        lax.psum_scatter(gate_part, "row", scatter_dimension=0, tiled=True),
        lax.psum_scatter(up_part, "row", scatter_dimension=0, tiled=True),
    )
    hidden_own = (jax.nn.silu(gate_own) * up_own).astype(jnp.bfloat16)
    hidden_all = lax.all_gather(hidden_own, "row", axis=0, tiled=True)
    result_part = jnp.dot(hidden_all, down_weight, preferred_element_type=jnp.float32)
    tok_col = inputs.shape[0]
    offset = lax.axis_index("col") * tok_col
    result_own = lax.psum_scatter(result_part, "col", scatter_dimension=0, tiled=True)
    target_own = lax.dynamic_slice_in_dim(target, offset, tok_col, 0)
    error_own = (result_own - target_own.astype(jnp.float32)).astype(jnp.bfloat16)
    output = result_own.astype(jnp.bfloat16)
    error_all = lax.all_gather(error_own, "col", axis=0, tiled=True)
    grad_down_weight = contract_first(hidden_all, error_all).astype(jnp.bfloat16)
    hidden_grad_part = contract_last(error_all, down_weight)
    hidden_grad = lax.psum_scatter(hidden_grad_part, "row", scatter_dimension=0, tiled=True)
    gate_grad_own, up_grad_own = gate_grads(hidden_grad, gate_own, up_own)
    gate_grad_all, up_grad_all = (
        lax.all_gather(gate_grad_own, "row", axis=0, tiled=True),
        lax.all_gather(up_grad_own, "row", axis=0, tiled=True),
    )
    grad_gate_weight = contract_first(tokens_all, gate_grad_all).astype(jnp.bfloat16)
    grad_up_weight = contract_first(tokens_all, up_grad_all).astype(jnp.bfloat16)
    input_grad_part = contract_last(gate_grad_all, gate_weight) + contract_last(
        up_grad_all, up_weight
    )
    grad_inputs = lax.psum_scatter(input_grad_part, "col", scatter_dimension=0, tiled=True).astype(
        jnp.bfloat16
    )
    return (output, grad_inputs, grad_gate_weight, grad_up_weight, grad_down_weight)


def solution(mesh):
    placed = (P("col", "row"), P(None, "row"), P("row", "col"), P("row", "col"), P("col", "row"))
    return jax.shard_map(
        body,
        mesh=mesh,
        in_specs=placed,
        out_specs=(
            P("col", "row"),
            P("col", "row"),
            P("row", "col"),
            P("row", "col"),
            P("col", "row"),
        ),
        check_vma=False,
    )
```

profile of v0, /device:TPU:4, one launch (start us, length us, event | category | flops | bytes accessed | tf_op | source)
XLA Modules:
  0.0 833.2 jit_solution(12145454576737987996)
XLA Ops:
  8.0 83.7 %all-gather.6.cloned.1.call-done = bf16[1024,1024]{1,0:T(8,128)(2,1)} async-done(((bf16[32,1024]{1,0:T(8,128)(2,1)}), bf16[1024,1024]{1,0:T(8,128)(2,1)}) %all-gather.6.cloned.1.call-update) | async-done | bytes 2097168 | tf_op jit(solution)/shard_map/all_gather | solution.py:30
  91.7 4.4 fusion.4
  97.7 3.8 fusion.3
  101.5 23.3 %reduce-scatter.8.cloned.1.call-done = f32[128,512]{1,0:T(8,128)} async-done(((f32[1024,512]{1,0:T(8,128)}), f32[128,512]{1,0:T(8,128)}) %reduce-scatter.8.cloned.1.call-update) | async-done | bytes 262160 | tf_op jit(solution)/shard_map/reduce_scatter | solution.py:35
  124.8 37.8 %reduce-scatter.6.cloned.1.call-done = f32[128,512]{1,0:T(8,128)} async-done(((f32[1024,512]{1,0:T(8,128)}), f32[128,512]{1,0:T(8,128)}) %reduce-scatter.6.cloned.1.call-update) | async-done | bytes 262160 | tf_op jit(solution)/shard_map/reduce_scatter | solution.py:34
  162.7 1.8 multiply_convert_fusion.2
  164.5 28.6 %all-gather.8.cloned.1.call-done = bf16[1024,512]{1,0:T(8,128)(2,1)} async-done(((bf16[128,512]{1,0:T(8,128)(2,1)}), bf16[1024,512]{1,0:T(8,128)(2,1)}) %all-gather.8.cloned.1.call-update) | async-done | bytes 1048592 | tf_op jit(solution)/shard_map/all_gather | solution.py:38
  193.1 4.4 fusion.5
  197.6 224.9 %reduce-scatter.10.cloned.1.call-done = f32[32,1024]{1,0:T(8,128)} async-done(((f32[1024,1024]{1,0:T(8,128)}), f32[32,1024]{1,0:T(8,128)}) %reduce-scatter.10.cloned.1.call-update) | async-done | bytes 131088 | tf_op jit(solution)/shard_map/reduce_scatter | solution.py:42
  422.5 1.7 subtract_convert_fusion
  424.2 77.6 %all-gather.10.cloned.1.call-done = bf16[1024,1024]{1,0:T(8,128)(2,1)} async-done(((bf16[32,1024]{1,0:T(8,128)(2,1)}), bf16[1024,1024]{1,0:T(8,128)(2,1)}) %all-gather.10.cloned.1.call-update) | async-done | bytes 2097168 | tf_op jit(solution)/shard_map/all_gather | solution.py:46
  501.8 4.2 fusion.6
  506.1 28.7 %reduce-scatter.12.cloned.1.call-done = f32[128,512]{1,0:T(8,128)} async-done(((f32[1024,512]{1,0:T(8,128)}), f32[128,512]{1,0:T(8,128)}) %reduce-scatter.12.cloned.1.call-update) | async-done | bytes 262160 | tf_op jit(solution)/shard_map/reduce_scatter | solution.py:49
  534.7 1.9 multiply_convert_fusion
  537.4 27.9 %all-gather.12.cloned.1.call-done = bf16[1024,512]{1,0:T(8,128)(2,1)} async-done(((bf16[128,512]{1,0:T(8,128)(2,1)}), bf16[1024,512]{1,0:T(8,128)(2,1)}) %all-gather.12.cloned.1.call-update) | async-done | bytes 1048592 | tf_op jit(solution)/shard_map/all_gather | solution.py:52
  565.4 4.8 fusion.7
  570.1 23.4 %all-gather.14.cloned.1.call-done = bf16[1024,512]{1,0:T(8,128)(2,1)} async-done(((bf16[128,512]{1,0:T(8,128)(2,1)}), bf16[1024,512]{1,0:T(8,128)(2,1)}) %all-gather.14.cloned.1.call-update) | async-done | bytes 1048592 | tf_op jit(solution)/shard_map/all_gather | solution.py:53
  593.5 6.1 convolution_add_fusion
  599.6 4.2 convolution_convert_fusion
  603.8 2.3 fusion.1
  606.1 2.3 copy.11
  608.4 3.5 fusion
  611.9 2.3 copy.10
  614.1 210.7 %reduce-scatter.14.cloned.1.call-done = f32[32,1024]{1,0:T(8,128)} async-done(((f32[1024,1024]{1,0:T(8,128)}), f32[32,1024]{1,0:T(8,128)}) %reduce-scatter.14.cloned.1.call-update) | async-done | bytes 131088 | tf_op jit(solution)/shard_map/reduce_scatter | solution.py:60
  (29 shorter events, 5.0 us)
Async XLA Ops:
  7.2 185.9 %copy-start = (bf16[512,1024]{1,0:T(8,128)(2,1)S(1)}, bf16[512,1024]{1,0:T(8,128)(2,1)}, u32[]{:S(2)}) copy-start(bf16[512,1024]{1,0:T(8,128)(2,1)} %param.9) | copy-start | bytes 3145732
  7.2 84.5 %all-gather.6.cloned.1.call-start = ((), (), s32[]{:S(2)}) async-start(), calls=%async_computation.5 | async-start | bytes 2162688 | tf_op jit(solution)/shard_map/all_gather | solution.py:30
  7.9 116.9 %reduce-scatter.8.cloned.1.call-start = ((), (), s32[]{:S(2)}) async-start(), calls=%async_computation.7 | async-start | bytes 2359296 | tf_op jit(solution)/shard_map/reduce_scatter | solution.py:35
  96.1 1.6 copy-start.1
  96.1 66.5 %reduce-scatter.6.cloned.1.call-start = ((), (), s32[]{:S(2)}) async-start(), calls=%async_computation.6 | async-start | bytes 2359296 | tf_op jit(solution)/shard_map/reduce_scatter | solution.py:34
  101.5 91.6 %all-gather.8.cloned.1.call-start = ((), (), s32[]{:S(2)}) async-start(), calls=%async_computation.8 | async-start | bytes 1179648 | tf_op jit(solution)/shard_map/all_gather | solution.py:38
  164.5 258.0 %reduce-scatter.10.cloned.1.call-start = ((), (), s32[]{:S(2)}) async-start(), calls=%async_computation.9 | async-start | bytes 4325376 | tf_op jit(solution)/shard_map/reduce_scatter | solution.py:42
  197.5 304.3 %all-gather.10.cloned.1.call-start = ((), (), s32[]{:S(2)}) async-start(), calls=%async_computation.10 | async-start | bytes 2162688 | tf_op jit(solution)/shard_map/all_gather | solution.py:46
  424.2 110.6 %reduce-scatter.12.cloned.1.call-start = ((), (), s32[]{:S(2)}) async-start(), calls=%async_computation.11 | async-start | bytes 2359296 | tf_op jit(solution)/shard_map/reduce_scatter | solution.py:49
  506.0 28.7 %copy-start.3 = (f32[128,512]{1,0:T(8,128)S(1)}, f32[128,512]{1,0:T(8,128)}, u32[]{:S(2)}) copy-start(f32[128,512]{1,0:T(8,128)} %reduce-scatter.8.cloned.1.call-done) | copy-start | bytes 786436
  506.0 59.3 %all-gather.12.cloned.1.call-start = ((), (), s32[]{:S(2)}) async-start(), calls=%async_computation.12 | async-start | bytes 1179648 | tf_op jit(solution)/shard_map/all_gather | solution.py:52
  536.6 56.9 %all-gather.14.cloned.1.call-start = ((), (), s32[]{:S(2)}) async-start(), calls=%async_computation.13 | async-start | bytes 1179648 | tf_op jit(solution)/shard_map/all_gather | solution.py:53
  537.4 287.5 %reduce-scatter.14.cloned.1.call-start = ((), (), s32[]{:S(2)}) async-start(), calls=%async_computation.14 | async-start | bytes 4325376 | tf_op jit(solution)/shard_map/reduce_scatter | solution.py:60
  599.6 4.2 copy-start.2
Sparse Core Ops, SparseCore 0:
  10.6 81.0 all-gather.5
  96.3 28.5 reduce-scatter.7
  127.4 35.2 reduce-scatter.5
  165.0 28.0 all-gather.7
  197.6 224.8 reduce-scatter.9
  425.5 76.2 all-gather.9
  506.1 28.5 reduce-scatter.11
  537.2 28.1 all-gather.11
  567.8 25.6 all-gather.13
  599.7 225.0 reduce-scatter.13
where the time goes:
time: 834 us; the launch traced here: 833 us
  waiting for transfers between devices  768 us (92%)
  matrix products  37.6 us (5%)
  between operations  14.2 us (2%)
    reduce_scatter x1, waiting for transfers between devices, body(): lax.psum_scatter(result_part, 'col', scatter_dimension=0, tiled=True)  225 us
    reduce_scatter x1, waiting for transfers between devices, body(): lax.psum_scatter(input_grad_part, 'col', scatter_dimension=0, tiled=True)  211 us
    all_gather x1, waiting for transfers between devices, body(): tokens_all = lax.all_gather(inputs, 'col', axis=0, tiled=True)  83.7 us
    all_gather x1, waiting for transfers between devices, body(): error_all = lax.all_gather(error_own, 'col', axis=0, tiled=True)  77.6 us
    reduce_scatter x1, waiting for transfers between devices, body(): lax.psum_scatter(gate_part, 'row', scatter_dimension=0, tiled=True)  37.8 us
    reduce_scatter x1, waiting for transfers between devices, body(): lax.psum_scatter(hidden_grad_part, 'row', scatter_dimension=0, tiled=True)  28.7 us
    all_gather x1, waiting for transfers between devices, body(): hidden_all = lax.all_gather(hidden_own, 'row', axis=0, tiled=True)  28.6 us
    all_gather x1, waiting for transfers between devices, body(): lax.all_gather(gate_grad_own, 'row', axis=0, tiled=True)  27.9 us
  transfers between devices with their start and end apart: 10, of which 10 were waited for; matrix products, arithmetic and copies ran while one was open for 3% of the time, Pallas kernels for 0%

commit v1 on v0

--- a/solution.py
+++ b/solution.py
@@ -43,7 +43,9 @@
     target_own = lax.dynamic_slice_in_dim(target, offset, tok_col, 0)
     error_own = (result_own - target_own.astype(jnp.float32)).astype(jnp.bfloat16)
     output = result_own.astype(jnp.bfloat16)
-    error_all = lax.all_gather(error_own, "col", axis=0, tiled=True)
+    error_all = jnp.concatenate(
+        lax.all_to_all(jnp.stack([error_own] * lax.axis_size("col")), "col", 0, 0), axis=0
+    )
     grad_down_weight = contract_first(hidden_all, error_all).astype(jnp.bfloat16)
     hidden_grad_part = contract_last(error_all, down_weight)
     hidden_grad = lax.psum_scatter(hidden_grad_part, "row", scatter_dimension=0, tiled=True)

time: 834 us -> 808 us (0.969)
  waiting for transfers between devices: 768 us -> 691 us
  blocking collectives: 0 us -> 52 us
    all_gather x1 -> x0, waiting for transfers between devices: 77.6 us -> none  [body(): error_all = lax.all_gather(error_own, 'col', axis=0, tiled=True)]
    all_to_all x0 -> x1, blocking collectives: none -> 52 us  [body(): lax.all_to_all(jnp.stack([error_own] * lax.axis_size('col')), 'col', 0, 0)]
  transfers between devices with their start and end apart: 10 -> 9, of which waited for: 10 -> 9; matrix products, arithmetic and copies ran while one was open for 3% -> 3% of each run, Pallas kernels for 0% -> 0%
where the time goes in v1:
time: 808 us; the launch traced here: 807 us
  waiting for transfers between devices  691 us (86%)
  blocking collectives  52 us (6%)
  matrix products  36.1 us (4%)
  between operations  13.9 us (2%)
    reduce_scatter x1, waiting for transfers between devices, body(): lax.psum_scatter(result_part, 'col', scatter_dimension=0, tiled=True)  225 us
    reduce_scatter x1, waiting for transfers between devices, body(): lax.psum_scatter(input_grad_part, 'col', scatter_dimension=0, tiled=True)  211 us
    all_gather x1, waiting for transfers between devices, body(): tokens_all = lax.all_gather(inputs, 'col', axis=0, tiled=True)  83.7 us
    all_to_all x1, blocking collectives, body(): lax.all_to_all(jnp.stack([error_own] * lax.axis_size('col')), 'col', 0, 0)  52 us
    reduce_scatter x1, waiting for transfers between devices, body(): lax.psum_scatter(gate_part, 'row', scatter_dimension=0, tiled=True)  37.8 us
    reduce_scatter x1, waiting for transfers between devices, body(): lax.psum_scatter(hidden_grad_part, 'row', scatter_dimension=0, tiled=True)  28.6 us
    all_gather x1, waiting for transfers between devices, body(): hidden_all = lax.all_gather(hidden_own, 'row', axis=0, tiled=True)  28.6 us
    all_gather x1, waiting for transfers between devices, body(): lax.all_gather(gate_grad_own, 'row', axis=0, tiled=True)  27.9 us
  transfers between devices with their start and end apart: 9, of which 9 were waited for; matrix products, arithmetic and copies ran while one was open for 3% of the time, Pallas kernels for 0%

profile of v1, /device:TPU:4, one launch (start us, length us, event | category | flops | bytes accessed | tf_op | source)
XLA Modules:
  0.0 807.4 jit_solution(14259323960396147954)
XLA Ops:
  8.0 83.7 %all-gather.5.cloned.1.call-done = bf16[1024,1024]{1,0:T(8,128)(2,1)} async-done(((bf16[32,1024]{1,0:T(8,128)(2,1)}), bf16[1024,1024]{1,0:T(8,128)(2,1)}) %all-gather.5.cloned.1.call-update) | async-done | bytes 2097168 | tf_op jit(solution)/shard_map/all_gather | solution.py:30
  91.7 4.4 fusion.4
  97.7 3.8 fusion.3
  101.6 23.3 %reduce-scatter.8.cloned.1.call-done = f32[128,512]{1,0:T(8,128)} async-done(((f32[1024,512]{1,0:T(8,128)}), f32[128,512]{1,0:T(8,128)}) %reduce-scatter.8.cloned.1.call-update) | async-done | bytes 262160 | tf_op jit(solution)/shard_map/reduce_scatter | solution.py:35
  124.9 37.8 %reduce-scatter.6.cloned.1.call-done = f32[128,512]{1,0:T(8,128)} async-done(((f32[1024,512]{1,0:T(8,128)}), f32[128,512]{1,0:T(8,128)}) %reduce-scatter.6.cloned.1.call-update) | async-done | bytes 262160 | tf_op jit(solution)/shard_map/reduce_scatter | solution.py:34
  162.7 1.8 multiply_convert_fusion.2
  164.5 28.6 %all-gather.7.cloned.1.call-done = bf16[1024,512]{1,0:T(8,128)(2,1)} async-done(((bf16[128,512]{1,0:T(8,128)(2,1)}), bf16[1024,512]{1,0:T(8,128)(2,1)}) %all-gather.7.cloned.1.call-update) | async-done | bytes 1048592 | tf_op jit(solution)/shard_map/all_gather | solution.py:38
  193.1 4.4 fusion.5
  197.6 225.1 %reduce-scatter.10.cloned.1.call-done = f32[32,1024]{1,0:T(8,128)} async-done(((f32[1024,1024]{1,0:T(8,128)}), f32[32,1024]{1,0:T(8,128)}) %reduce-scatter.10.cloned.1.call-update) | async-done | bytes 131088 | tf_op jit(solution)/shard_map/reduce_scatter | solution.py:42
  422.7 1.6 subtract_convert_fusion
  424.6 52.0 %all_to_all.5 = bf16[32,32,1024]{2,1,0:T(8,128)(2,1)S(1)} all-to-all(bf16[32,32,1024]{2,1,0:T(8,128)(2,1)S(1)} %stack.2), channel_id=1, replica_groups=mesh['row'=8,'col'=32] {'col'}, dimensions={0} | all-to-all | bytes 4194304 | tf_op jit(solution)/shard_map/all_to_all | solution.py:47
  477.9 2.6 fusion.6
  480.6 28.6 %reduce-scatter.12.cloned.1.call-done = f32[128,512]{1,0:T(8,128)} async-done(((f32[1024,512]{1,0:T(8,128)}), f32[128,512]{1,0:T(8,128)}) %reduce-scatter.12.cloned.1.call-update) | async-done | bytes 262160 | tf_op jit(solution)/shard_map/reduce_scatter | solution.py:51
  509.2 1.9 multiply_convert_fusion
  511.8 27.9 %all-gather.9.cloned.1.call-done = bf16[1024,512]{1,0:T(8,128)(2,1)} async-done(((bf16[128,512]{1,0:T(8,128)(2,1)}), bf16[1024,512]{1,0:T(8,128)(2,1)}) %all-gather.9.cloned.1.call-update) | async-done | bytes 1048592 | tf_op jit(solution)/shard_map/all_gather | solution.py:54
  539.8 4.8 fusion.7
  544.6 23.4 %all-gather.11.cloned.1.call-done = bf16[1024,512]{1,0:T(8,128)(2,1)} async-done(((bf16[128,512]{1,0:T(8,128)(2,1)}), bf16[1024,512]{1,0:T(8,128)(2,1)}) %all-gather.11.cloned.1.call-update) | async-done | bytes 1048592 | tf_op jit(solution)/shard_map/all_gather | solution.py:55
  567.9 6.1 convolution_add_fusion
  574.0 4.2 convolution_convert_fusion
  578.3 2.3 fusion.1
  580.5 2.3 copy.11
  582.8 3.5 fusion
  586.3 2.3 copy.10
  588.6 210.8 %reduce-scatter.14.cloned.1.call-done = f32[32,1024]{1,0:T(8,128)} async-done(((f32[1024,1024]{1,0:T(8,128)}), f32[32,1024]{1,0:T(8,128)}) %reduce-scatter.14.cloned.1.call-update) | async-done | bytes 131088 | tf_op jit(solution)/shard_map/reduce_scatter | solution.py:62
  (30 shorter events, 6.5 us)
Async XLA Ops:
  7.2 185.9 %copy-start = (bf16[512,1024]{1,0:T(8,128)(2,1)S(1)}, bf16[512,1024]{1,0:T(8,128)(2,1)}, u32[]{:S(2)}) copy-start(bf16[512,1024]{1,0:T(8,128)(2,1)} %param.9) | copy-start | bytes 3145732
  7.2 84.5 %all-gather.5.cloned.1.call-start = ((), (), s32[]{:S(2)}) async-start(), calls=%async_computation.6 | async-start | bytes 2162688 | tf_op jit(solution)/shard_map/all_gather | solution.py:30
  7.9 116.9 %reduce-scatter.8.cloned.1.call-start = ((), (), s32[]{:S(2)}) async-start(), calls=%async_computation.8 | async-start | bytes 2359296 | tf_op jit(solution)/shard_map/reduce_scatter | solution.py:35
  96.1 1.6 copy-start.1
  96.1 66.5 %reduce-scatter.6.cloned.1.call-start = ((), (), s32[]{:S(2)}) async-start(), calls=%async_computation.7 | async-start | bytes 2359296 | tf_op jit(solution)/shard_map/reduce_scatter | solution.py:34
  101.5 91.6 %all-gather.7.cloned.1.call-start = ((), (), s32[]{:S(2)}) async-start(), calls=%async_computation.9 | async-start | bytes 1179648 | tf_op jit(solution)/shard_map/all_gather | solution.py:38
  164.5 258.2 %reduce-scatter.10.cloned.1.call-start = ((), (), s32[]{:S(2)}) async-start(), calls=%async_computation.10 | async-start | bytes 4325376 | tf_op jit(solution)/shard_map/reduce_scatter | solution.py:42
  197.5 311.6 %reduce-scatter.12.cloned.1.call-start = ((), (), s32[]{:S(2)}) async-start(), calls=%async_computation.11 | async-start | bytes 2359296 | tf_op jit(solution)/shard_map/reduce_scatter | solution.py:51
  476.5 1.4 copy-start.2
  480.5 28.7 %copy-start.4 = (f32[128,512]{1,0:T(8,128)S(1)}, f32[128,512]{1,0:T(8,128)}, u32[]{:S(2)}) copy-start(f32[128,512]{1,0:T(8,128)} %reduce-scatter.8.cloned.1.call-done) | copy-start | bytes 786436
  480.5 59.3 %all-gather.9.cloned.1.call-start = ((), (), s32[]{:S(2)}) async-start(), calls=%async_computation.12 | async-start | bytes 1179648 | tf_op jit(solution)/shard_map/all_gather | solution.py:54
  511.0 56.9 %all-gather.11.cloned.1.call-start = ((), (), s32[]{:S(2)}) async-start(), calls=%async_computation.13 | async-start | bytes 1179648 | tf_op jit(solution)/shard_map/all_gather | solution.py:55
  511.8 287.5 %reduce-scatter.14.cloned.1.call-start = ((), (), s32[]{:S(2)}) async-start(), calls=%async_computation.14 | async-start | bytes 4325376 | tf_op jit(solution)/shard_map/reduce_scatter | solution.py:62
  574.0 4.2 copy-start.3
Sparse Core Ops, SparseCore 0:
  10.6 81.0 all-gather.4
  96.3 28.5 reduce-scatter.7
  127.4 35.2 reduce-scatter.5
  165.0 28.0 all-gather.6
  197.7 224.9 reduce-scatter.9
  480.7 28.4 reduce-scatter.11
  511.6 28.1 all-gather.8
  542.2 25.6 all-gather.10
  574.2 225.1 reduce-scatter.13
